TPU v7x, 32 devices: a whole 2x2x4 slice. The times are simulated.
32 devices in a mesh: mem: 4 (over z), tile: 8 (over y, x, core).
Axes of the slice: x: 2, y: 2, z: 4, core: 2. Of those that a mesh axis runs over, the one named last changes fastest.
Arguments:
- alpha: float32 [32, 8, 192, 384], P('mem', None, 'tile'), may hold values from -6 to 6
- ensemble: bfloat16 [2, 32, 8, 192, 384], P(None, 'mem', None, 'tile'), may hold values from -1 to 1
- innovation: float32 [2, 8, 192, 384], P(None, None, 'tile'), may hold values from -6 to 6
- precision: float32 [2, 8, 192, 384], P(None, None, 'tile'), may hold values from 0.5 to 8
- diffusivity: float32 [2, 8, 192, 384], P(None, None, 'tile'), may hold values from 0.01 to 0.48, as said below
Outputs:
- gradient: float32 [32, 8, 192, 384], P('mem', None, 'tile')
- increment: float32 [2, 8, 192, 384], P(None, None, 'tile')
Inputs may be any that keep to these rules, and one draw needn't show every extreme that they name: diffusivity[0] lies between 0.40 and 0.48 and diffusivity[1] between 0.01 and 0.02, so the four faces of a cell sum to at most 1.
All inputs are finite; a program needn't handle non-finite values.
Results may differ from a plain program's by a relative error of at most 0.0003.
Values sent between devices are 32-bit elements; how exact they have to be, the bound alone decides.
A program may use at most 64 MiB of HBM per device.

v0:
```python
import jax
import jax.numpy as jnp
from jax import lax
from jax.sharding import PartitionSpec as P

STEPS = 4


def extended(cells, sides, width):
    for axis, dim in sides:
        count = lax.axis_size(axis)
        head = lax.slice_in_dim(cells, 0, width, axis=dim)
        tail = lax.slice_in_dim(cells, cells.shape[dim] - width, cells.shape[dim], axis=dim)
        cells = jnp.concatenate(
            [
                lax.ppermute(tail, axis, [(i, (i + 1) % count) for i in range(count)]),
                cells,
                lax.ppermute(head, axis, [((i + 1) % count, i) for i in range(count)]),
            ],
            axis=dim,
        )
    return cells


def diffuse(field, coeffs, width):
    for sweep in range(width):
        columns = field.shape[2]
        zonal_face = coeffs[0, :, sweep : sweep + columns - 1]
        merid_face = coeffs[1, :, sweep + 1 : sweep + columns - 1]
        zonal_flux = zonal_face * (field[:, :, 1:] - field[:, :, :-1])
        interior = field[:, :, 1:-1]
        merid_flux = merid_face[:, :, :-1] * (interior[:, :, :, 1:] - interior[:, :, :, :-1])
        padding = jnp.zeros_like(interior[:, :, :, :1])
        north_flux = jnp.concatenate([merid_flux, padding], axis=3)
        south_flux = jnp.concatenate([padding, merid_flux], axis=3)
        field = interior + zonal_flux[:, :, 1:] - zonal_flux[:, :, :-1] + north_flux - south_flux
    return field


def per_device(alpha, ensemble, innovation, precision, diffusivity):
    coeffs = extended(diffusivity, (("tile", 2),), STEPS)
    padded = extended(alpha, (("tile", 2),), STEPS)
    localized = diffuse(padded, coeffs, STEPS)
    partial_sum = jnp.sum(ensemble.astype(jnp.float32) * localized[None], axis=1)
    increment = lax.psum(partial_sum, "mem")
    weighted = precision * (increment - innovation)
    projected = jnp.sum(ensemble.astype(jnp.float32) * weighted[:, None], axis=0)
    padded_adj = extended(projected, (("tile", 2),), STEPS)
    adjoint_field = diffuse(padded_adj, coeffs, STEPS)
    gradient = alpha + adjoint_field
    return (gradient, increment)


def solution(mesh):
    in_specs = (
        P("mem", None, "tile", None),
        P(None, "mem", None, "tile", None),
        P(None, None, "tile", None),
        P(None, None, "tile", None),
        P(None, None, "tile", None),
    )
    out_specs = (P("mem", None, "tile", None), P(None, None, "tile", None))
    return jax.shard_map(
        per_device, mesh=mesh, in_specs=in_specs, out_specs=out_specs, check_vma=False
    )
```

profile of v0, /device:TPU:1, one launch (start us, length us, event | category | flops | bytes accessed | tf_op | source)
XLA Modules:
  0.0 121.3 jit_solution(3033836365526358352)
XLA Ops:
  7.2 1.1 fusion.38
  8.3 2.6 %collective-permute-start.2 = (f32[2,8,4,384]{3,2,1,0:T(4,128)S(1)}, f32[2,8,4,384]{3,2,1,0:T(4,128)S(1)}, u32[]{:S(2)}, u32[]{:S(2)}) collective-permute-start(f32[2,8,4,384]{3,2,1,0:T(4,128)S(1)} %get-tuple-element.8), channel_id=1, source_target_pairs={{0,1},{1,2},{2,3},{3,4},{4,5},{5,6},{6,7},{7,0},{8,9},{9,10},{10,1... | collective-permute-start | bytes 294920 | tf_op jit(solution)/shard_map/ppermute | solution.py:16
  11.0 1.5 %fusion.37 = (f32[8,8,4,384]{3,2,1,0:T(4,128)S(1)}, f32[8,8,4,384]{3,2,1,0:T(4,128)S(1)}) fusion(f32[8,8,24,384]{3,2,1,0:T(8,128)} %param.5), kind=kLoop, calls=%fused_computation.83 | loop fusion | bytes 1572864 | tf_op jit(solution)/shard_map/slice | solution.py:13
  12.5 1.8 %collective-permute-start = (f32[8,8,4,384]{3,1,2,0:T(8,128)S(1)}, f32[8,8,4,384]{3,1,2,0:T(8,128)S(1)}, u32[]{:S(2)}, u32[]{:S(2)}) collective-permute-start(f32[8,8,4,384]{3,1,2,0:T(8,128)S(1)} %copy.29), channel_id=1, source_target_pairs={{0,1},{1,2},{2,3},{3,4},{4,5},{5,6},{6,7},{7,0},{8,9},{9,10},{10,1... | collective-permute-start | bytes 1179656 | tf_op jit(solution)/shard_map/ppermute | solution.py:16
  15.5 0.8 slice_bitcast_fusion.2
  17.0 0.8 slice_bitcast_fusion
  17.9 0.8 slice_bitcast_fusion.1
  18.6 2.6 %collective-permute-done = f32[8,8,4,384]{3,1,2,0:T(8,128)S(1)} collective-permute-done((f32[8,8,4,384]{3,1,2,0:T(8,128)S(1)}, f32[8,8,4,384]{3,1,2,0:T(8,128)S(1)}, u32[]{:S(2)}, u32[]{:S(2)}) %collective-permute-start) | collective-permute-done | bytes 393248 | tf_op jit(solution)/shard_map/ppermute | solution.py:16
  21.4 4.5 %collective-permute-done.1 = f32[8,8,4,384]{3,1,2,0:T(8,128)S(1)} collective-permute-done((f32[8,8,4,384]{3,1,2,0:T(8,128)S(1)}, f32[8,8,4,384]{3,1,2,0:T(8,128)S(1)}, u32[]{:S(2)}, u32[]{:S(2)}) %collective-permute-start.1) | collective-permute-done | bytes 393248 | tf_op jit(solution)/shard_map/ppermute | solution.py:18
  26.5 1.2 fusion.24
  28.2 1.7 %fusion.26 = f32[8,8,30,384]{3,2,1,0:T(8,128)S(1)} fusion(f32[8,8,31,384]{3,2,1,0:T(8,128)S(1)} %fusion.27, f32[8,8,32,384]{3,2,1,0:T(8,128)S(1)} %pad_maximum_fusion, f32[8,8,30,383]{3,2,1,0:T(8,128)S(1)} %fusion.24), kind=kLoop, calls=%fused_computation.52 | loop fusion | flops 2949120 | bytes 14737920 | tf_op jit(solution)/shard_map/sub | solution.py:36
  29.9 1.2 fusion.20
  31.7 1.7 %fusion.22 = f32[8,8,28,384]{3,2,1,0:T(8,128)S(1)} fusion(f32[8,8,29,384]{3,2,1,0:T(8,128)S(1)} %fusion.23, f32[8,8,30,384]{3,2,1,0:T(8,128)S(1)} %fusion.26, f32[8,8,28,383]{3,2,1,0:T(8,128)S(1)} %fusion.20), kind=kLoop, calls=%fused_computation.44 | loop fusion | flops 2752512 | bytes 13755392 | tf_op jit(solution)/shard_map/sub | solution.py:36
  33.4 1.2 fusion.16
  35.2 1.7 %fusion.18 = f32[8,8,26,384]{3,2,1,0:T(8,128)S(1)} fusion(f32[8,8,27,384]{3,2,1,0:T(8,128)S(1)} %fusion.19, f32[8,8,28,384]{3,2,1,0:T(8,128)S(1)} %fusion.22, f32[8,8,26,383]{3,2,1,0:T(8,128)S(1)} %fusion.16), kind=kLoop, calls=%fused_computation.36 | loop fusion | flops 2555904 | bytes 12772864 | tf_op jit(solution)/shard_map/sub | solution.py:36
  37.8 1.1 fusion.32
  38.9 1.2 fusion.34
  40.6 1.3 %fusion = f32[2,8,24,384]{3,2,1,0:T(8,128)} fusion(bf16[2,8,8,24,384]{4,3,2,1,0:T(8,128)(2,1)S(1)} %copy-done.1, f32[8,8,24,384]{3,2,1,0:T(8,128)S(1)} %fusion.34), kind=kLoop, calls=%fused_computation.2 | loop fusion | flops 3391488 | bytes 5308416 | tf_op jit(solution)/shard_map/reduce_sum | solution.py:44
  41.9 39.6 %all-reduce.18.cloned.1.call-done = f32[2,8,24,384]{3,2,1,0:T(8,128)} async-done(((f32[2,8,24,384]{3,2,1,0:T(8,128)}), f32[2,8,24,384]{3,2,1,0:T(8,128)}) %all-reduce.18.cloned.1.call-update) | async-done | bytes 589840 | tf_op jit(solution)/shard_map/psum | solution.py:45
  81.5 1.6 %subtract_multiply_fusion = f32[2,8,24,384]{3,2,1,0:T(8,128)S(1)} fusion(f32[2,8,24,384]{3,2,1,0:T(8,128)} %param.8, f32[2,8,24,384]{3,2,1,0:T(8,128)} %all-reduce.18.cloned.1.call-done, f32[2,8,24,384]{3,2,1,0:T(8,128)} %param.7), kind=kLoop, calls=%fused_computation.72 | loop fusion | flops 294912 | bytes 2359296 | tf_op jit(solution)/shard_map/mul | solution.py:46
  84.4 2.4 %collective-permute-start.4 = (f32[8,8,4,384]{3,1,2,0:T(8,128)S(1)}, f32[8,8,4,384]{3,1,2,0:T(8,128)S(1)}, u32[]{:S(2)}, u32[]{:S(2)}) collective-permute-start(f32[8,8,4,384]{3,1,2,0:T(8,128)S(1)} %copy.25), channel_id=1, source_target_pairs={{0,1},{1,2},{2,3},{3,4},{4,5},{5,6},{6,7},{7,0},{8,9},{9,10},{10,1... | collective-permute-start | bytes 1179656 | tf_op jit(solution)/shard_map/ppermute | solution.py:16
  87.0 7.0 %collective-permute-done.4 = f32[8,8,4,384]{3,1,2,0:T(8,128)S(1)} collective-permute-done((f32[8,8,4,384]{3,1,2,0:T(8,128)S(1)}, f32[8,8,4,384]{3,1,2,0:T(8,128)S(1)}, u32[]{:S(2)}, u32[]{:S(2)}) %collective-permute-start.4) | collective-permute-done | bytes 393248 | tf_op jit(solution)/shard_map/ppermute | solution.py:16
  94.1 3.4 %collective-permute-done.5 = f32[8,8,4,384]{3,1,2,0:T(8,128)S(1)} collective-permute-done((f32[8,8,4,384]{3,1,2,0:T(8,128)S(1)}, f32[8,8,4,384]{3,1,2,0:T(8,128)S(1)}, u32[]{:S(2)}, u32[]{:S(2)}) %collective-permute-start.5) | collective-permute-done | bytes 393248 | tf_op jit(solution)/shard_map/ppermute | solution.py:18
  98.5 1.2 fusion.11
  100.2 1.7 %fusion.13 = f32[8,8,30,384]{3,2,1,0:T(8,128)S(1)} fusion(f32[8,8,31,384]{3,2,1,0:T(8,128)S(1)} %fusion.14, f32[8,8,32,384]{3,2,1,0:T(8,128)S(1)} %pad_maximum_fusion.1, f32[8,8,30,383]{3,2,1,0:T(8,128)S(1)} %fusion.11), kind=kLoop, calls=%fused_computation.26 | loop fusion | flops 2949120 | bytes 14737920 | tf_op jit(solution)/shard_map/sub | solution.py:36
  102.0 1.2 fusion.7
  103.7 1.7 %fusion.9 = f32[8,8,28,384]{3,2,1,0:T(8,128)S(1)} fusion(f32[8,8,29,384]{3,2,1,0:T(8,128)S(1)} %fusion.10, f32[8,8,30,384]{3,2,1,0:T(8,128)S(1)} %fusion.13, f32[8,8,28,383]{3,2,1,0:T(8,128)S(1)} %fusion.7), kind=kLoop, calls=%fused_computation.18 | loop fusion | flops 2752512 | bytes 13755392 | tf_op jit(solution)/shard_map/sub | solution.py:36
  105.4 1.2 fusion.3
  107.2 1.7 %fusion.5 = f32[8,8,26,384]{3,2,1,0:T(8,128)S(1)} fusion(f32[8,8,27,384]{3,2,1,0:T(8,128)S(1)} %fusion.6, f32[8,8,28,384]{3,2,1,0:T(8,128)S(1)} %fusion.9, f32[8,8,26,383]{3,2,1,0:T(8,128)S(1)} %fusion.3), kind=kLoop, calls=%fused_computation.10 | loop fusion | flops 2555904 | bytes 12772864 | tf_op jit(solution)/shard_map/sub | solution.py:36
  109.8 0.9 fusion.28
  110.8 2.9 %fusion.31 = f32[8,8,24,384]{3,2,1,0:T(8,128)} fusion(f32[8,8,24,384]{3,2,1,0:T(8,128)S(1)} %copy-done, f32[8,8,25,384]{3,2,1,0:T(8,128)S(1)} %fusion.2, f32[8,8,26,384]{3,2,1,0:T(8,128)S(1)} %fusion.5, f32[8,8,24,383]{3,2,1,0:T(8,128)S(1)} %fusion.28), kind=kLoop, calls=%fused_computation.63 | loop fusion | flops 2949120 | bytes 14149632 | tf_op jit(solution)/shard_map/add | solution.py:50
  113.7 0.8 copy.32
  (67 shorter events, 10.8 us)
Async XLA Ops:
  7.2 7.3 %copy-start.3 = (f32[2,8,24,384]{3,2,1,0:T(8,128)S(1)}, f32[2,8,24,384]{3,2,1,0:T(8,128)}, u32[]{:S(2)}) copy-start(f32[2,8,24,384]{3,2,1,0:T(8,128)} %param.9) | copy-start | bytes 1769476
  7.2 74.3 %all-reduce.18.cloned.1.call-start = ((), (), s32[]{:S(2)}) async-start(), calls=%async_computation | async-start | bytes 1179648 | tf_op jit(solution)/shard_map/psum | solution.py:45
  8.3 6.9 %collective-permute-start.2 = (f32[2,8,4,384]{3,2,1,0:T(4,128)S(1)}, f32[2,8,4,384]{3,2,1,0:T(4,128)S(1)}, u32[]{:S(2)}, u32[]{:S(2)}) collective-permute-start(f32[2,8,4,384]{3,2,1,0:T(4,128)S(1)} %get-tuple-element.8), channel_id=1, source_target_pairs={{0,1},{1,2},{2,3},{3,4},{4,5},{5,6},{6,7},{7,0},{8,9},{9,10},{10,1... | collective-permute-start | bytes 294920 | tf_op jit(solution)/shard_map/ppermute | solution.py:16
  11.0 4.3 %collective-permute-start.3 = (f32[2,8,4,384]{3,2,1,0:T(4,128)S(1)}, f32[2,8,4,384]{3,2,1,0:T(4,128)S(1)}, u32[]{:S(2)}, u32[]{:S(2)}) collective-permute-start(f32[2,8,4,384]{3,2,1,0:T(4,128)S(1)} %get-tuple-element.9), channel_id=1, source_target_pairs={{1,0},{2,1},{3,2},{4,3},{5,4},{6,5},{7,6},{0,7},{9,8},{10,9},{11,1... | collective-permute-start | bytes 294920 | tf_op jit(solution)/shard_map/ppermute | solution.py:18
  12.5 8.7 %collective-permute-start = (f32[8,8,4,384]{3,1,2,0:T(8,128)S(1)}, f32[8,8,4,384]{3,1,2,0:T(8,128)S(1)}, u32[]{:S(2)}, u32[]{:S(2)}) collective-permute-start(f32[8,8,4,384]{3,1,2,0:T(8,128)S(1)} %copy.29), channel_id=1, source_target_pairs={{0,1},{1,2},{2,3},{3,4},{4,5},{5,6},{6,7},{7,0},{8,9},{9,10},{10,1... | collective-permute-start | bytes 1179656 | tf_op jit(solution)/shard_map/ppermute | solution.py:16
  14.4 11.5 %collective-permute-start.1 = (f32[8,8,4,384]{3,1,2,0:T(8,128)S(1)}, f32[8,8,4,384]{3,1,2,0:T(8,128)S(1)}, u32[]{:S(2)}, u32[]{:S(2)}) collective-permute-start(f32[8,8,4,384]{3,1,2,0:T(8,128)S(1)} %copy.30), channel_id=1, source_target_pairs={{1,0},{2,1},{3,2},{4,3},{5,4},{6,5},{7,6},{0,7},{9,8},{10,9},{11,1... | collective-permute-start | bytes 1179656 | tf_op jit(solution)/shard_map/ppermute | solution.py:18
  15.4 11.1 %copy-start.12 = (f32[8,30,384]{2,1,0:T(8,128)}, f32[8,30,384]{2,1,0:T(8,128)S(1)}, u32[]{:S(2)}) copy-start(f32[8,30,384]{2,1,0:T(8,128)S(1)} %slice_bitcast_fusion.4) | copy-start | bytes 1105924
  15.4 10.5 %copy-start = (f32[8,8,24,384]{3,2,1,0:T(8,128)S(1)}, f32[8,8,24,384]{3,2,1,0:T(8,128)}, u32[]{:S(2)}) copy-start(f32[8,8,24,384]{3,2,1,0:T(8,128)} %param.5) | copy-start | bytes 7077892
  15.5 12.2 %copy-start.10 = (f32[8,31,384]{2,1,0:T(8,128)}, f32[8,31,384]{2,1,0:T(8,128)S(1)}, u32[]{:S(2)}) copy-start(f32[8,31,384]{2,1,0:T(8,128)S(1)} %slice_bitcast_fusion.5) | copy-start | bytes 1142788
  28.2 1.7 %copy-start.9 = (f32[8,28,384]{2,1,0:T(8,128)S(1)}, f32[8,28,384]{2,1,0:T(8,128)}, u32[]{:S(2)}) copy-start(f32[8,28,384]{2,1,0:T(8,128)} %slice_bitcast_fusion.2) | copy-start | bytes 1032196
  29.9 1.2 copy-start.7
  31.7 1.7 %copy-start.4 = (f32[8,26,384]{2,1,0:T(8,128)S(1)}, f32[8,26,384]{2,1,0:T(8,128)}, u32[]{:S(2)}) copy-start(f32[8,26,384]{2,1,0:T(8,128)} %slice_bitcast_fusion) | copy-start | bytes 958468
  33.4 1.2 copy-start.5
  36.9 1.0 copy-start.14
  38.9 1.7 %copy-start.1 = (bf16[2,8,8,24,384]{4,3,2,1,0:T(8,128)(2,1)S(1)}, bf16[2,8,8,24,384]{4,3,2,1,0:T(8,128)(2,1)}, u32[]{:S(2)}) copy-start(bf16[2,8,8,24,384]{4,3,2,1,0:T(8,128)(2,1)} %param.6) | copy-start | bytes 7077892
  81.5 2.2 %copy-start.2 = (bf16[2,8,8,24,384]{4,3,2,1,0:T(8,128)(2,1)S(1)}, bf16[2,8,8,24,384]{4,3,2,1,0:T(8,128)(2,1)}, u32[]{:S(2)}) copy-start(bf16[2,8,8,24,384]{4,3,2,1,0:T(8,128)(2,1)} %param.6) | copy-start | bytes 7077892
  84.4 9.5 %collective-permute-start.4 = (f32[8,8,4,384]{3,1,2,0:T(8,128)S(1)}, f32[8,8,4,384]{3,1,2,0:T(8,128)S(1)}, u32[]{:S(2)}, u32[]{:S(2)}) collective-permute-start(f32[8,8,4,384]{3,1,2,0:T(8,128)S(1)} %copy.25), channel_id=1, source_target_pairs={{0,1},{1,2},{2,3},{3,4},{4,5},{5,6},{6,7},{7,0},{8,9},{9,10},{10,1... | collective-permute-start | bytes 1179656 | tf_op jit(solution)/shard_map/ppermute | solution.py:16
  86.9 10.5 %collective-permute-start.5 = (f32[8,8,4,384]{3,1,2,0:T(8,128)S(1)}, f32[8,8,4,384]{3,1,2,0:T(8,128)S(1)}, u32[]{:S(2)}, u32[]{:S(2)}) collective-permute-start(f32[8,8,4,384]{3,1,2,0:T(8,128)S(1)} %copy.26), channel_id=1, source_target_pairs={{1,0},{2,1},{3,2},{4,3},{5,4},{6,5},{7,6},{0,7},{9,8},{10,9},{11,1... | collective-permute-start | bytes 1179656 | tf_op jit(solution)/shard_map/ppermute | solution.py:18
  97.5 1.0 copy-start.13
  98.5 1.2 copy-start.11
  102.0 1.2 copy-start.8
  105.4 1.2 copy-start.6
  108.9 1.0 copy-start.15
  110.8 2.9 %copy-start.16 = (f32[2,8,24,384]{3,2,1,0:T(8,128)S(1)}, f32[2,8,24,384]{3,2,1,0:T(8,128)}, u32[]{:S(2)}) copy-start(f32[2,8,24,384]{3,2,1,0:T(8,128)} %all-reduce.18.cloned.1.call-done) | copy-start | bytes 1769476
Sparse Core Ops, SparseCore 0:
  42.1 39.3 all-reduce.17
where the time goes:
time: 122 us; the launch traced here: 121 us
  waiting for transfers between devices  57 us (47%)
  other arithmetic  32.3 us (26%)
  between operations  14.5 us (12%)
  local copies, waits for them, and re-layouts  10.5 us (9%)
  starting transfers between devices  7.02 us (6%)
    psum x1, waiting for transfers between devices, per_device(): increment = lax.psum(partial_sum, 'mem')  39.6 us
    sub x7, other arithmetic, diffuse(): interior + zonal_flux[:, :, 1:] - zonal_flux[:, :, :-1] + north_flux  11.5 us
    ppermute x3, waiting for transfers between devices, extended(): lax.ppermute(tail, axis, [(i, (i + 1) % count) for i in range(count)])  9.61 us
    mul x8, other arithmetic, diffuse(): merid_face[:, :, :-1] * (interior[:, :, :, 1:] - interior[:, :, :, :-1])  9.07 us
    ppermute x3, waiting for transfers between devices, extended(): lax.ppermute(head, axis, [((i + 1) % count, i) for i in range(count)])  7.86 us
    ppermute x3, starting transfers between devices, extended(): lax.ppermute(tail, axis, [(i, (i + 1) % count) for i in range(count)])  6.86 us
    mul x9, other arithmetic, diffuse(): zonal_flux = zonal_face * (field[:, :, 1:] - field[:, :, :-1])  4.23 us
    unnamed x37, local copies, waits for them, and re-layouts  3.27 us
  transfers between devices with their start and end apart: 7, of which 5 were waited for; matrix products, arithmetic and copies ran while one was open for 5% of the time, Pallas kernels for 0%

commit v1 on v0

--- a/solution.py
+++ b/solution.py
@@ -42,7 +42,11 @@
     padded = extended(alpha, (("tile", 2),), STEPS)
     localized = diffuse(padded, coeffs, STEPS)
     partial_sum = jnp.sum(ensemble.astype(jnp.float32) * localized[None], axis=1)
-    increment = lax.psum(partial_sum, "mem")
+
+    def _search_skins(chip_axis, body):
+        return jax.lax.all_gather(body, axis_name=chip_axis).sum(axis=0)
+
+    increment = _search_skins("mem", partial_sum)
     weighted = precision * (increment - innovation)
     projected = jnp.sum(ensemble.astype(jnp.float32) * weighted[:, None], axis=0)
     padded_adj = extended(projected, (("tile", 2),), STEPS)

time: 122 us -> 134 us (1.098)
  waiting for transfers between devices: 57 us -> 67.8 us
  other arithmetic: 32.3 us -> 34.9 us
    all_gather x0 -> x1, waiting for transfers between devices: none -> 50.4 us  [_search_skins(): return jax.lax.all_gather(body, axis_name=chip_axis).sum(axis=0)]
    psum x1 -> x0, waiting for transfers between devices: 39.6 us -> none  [per_device(): increment = lax.psum(partial_sum, 'mem')]
    reduce_sum x0 -> x1, other arithmetic: none -> 2.67 us  [_search_skins(): return jax.lax.all_gather(body, axis_name=chip_axis).sum(axis=0)]
    unnamed x37 -> x34, local copies, waits for them, and re-layouts: 3.27 us -> 2.46 us
  transfers between devices with their start and end apart: 7 -> 7, of which waited for: 5 -> 5; matrix products, arithmetic and copies ran while one was open for 5% -> 4% of each run, Pallas kernels for 0% -> 0%
where the time goes in v1:
time: 134 us; the launch traced here: 133 us
  waiting for transfers between devices  67.8 us (51%)
  other arithmetic  34.9 us (26%)
  between operations  14.5 us (11%)
  local copies, waits for them, and re-layouts  9.67 us (7%)
  starting transfers between devices  6.56 us (5%)
    all_gather x1, waiting for transfers between devices, _search_skins(): return jax.lax.all_gather(body, axis_name=chip_axis).sum(axis=0)  50.4 us
    sub x7, other arithmetic, diffuse(): interior + zonal_flux[:, :, 1:] - zonal_flux[:, :, :-1] + north_flux  11.5 us
    ppermute x3, waiting for transfers between devices, extended(): lax.ppermute(tail, axis, [(i, (i + 1) % count) for i in range(count)])  9.6 us
    mul x8, other arithmetic, diffuse(): merid_face[:, :, :-1] * (interior[:, :, :, 1:] - interior[:, :, :, :-1])  9.07 us
    ppermute x3, waiting for transfers between devices, extended(): lax.ppermute(head, axis, [((i + 1) % count, i) for i in range(count)])  7.87 us
    ppermute x3, starting transfers between devices, extended(): lax.ppermute(tail, axis, [(i, (i + 1) % count) for i in range(count)])  6.4 us
    mul x9, other arithmetic, diffuse(): zonal_flux = zonal_face * (field[:, :, 1:] - field[:, :, :-1])  4.23 us
    add x1, other arithmetic, per_device(): gradient = alpha + adjoint_field  2.88 us
  transfers between devices with their start and end apart: 7, of which 5 were waited for; matrix products, arithmetic and copies ran while one was open for 4% of the time, Pallas kernels for 0%

profile of v1, /device:TPU:1, one launch (start us, length us, event | category | flops | bytes accessed | tf_op | source)
XLA Modules:
  0.0 133.5 jit_solution(4673400745367270359)
XLA Ops:
  7.2 1.1 fusion.38
  8.3 2.6 %collective-permute-start.2 = (f32[2,8,4,384]{3,2,1,0:T(4,128)S(1)}, f32[2,8,4,384]{3,2,1,0:T(4,128)S(1)}, u32[]{:S(2)}, u32[]{:S(2)}) collective-permute-start(f32[2,8,4,384]{3,2,1,0:T(4,128)S(1)} %get-tuple-element.8), channel_id=1, source_target_pairs={{0,1},{1,2},{2,3},{3,4},{4,5},{5,6},{6,7},{7,0},{8,9},{9,10},{10,1... | collective-permute-start | bytes 294920 | tf_op jit(solution)/shard_map/ppermute | solution.py:16
  11.0 1.5 %fusion.37 = (f32[8,8,4,384]{3,2,1,0:T(4,128)S(1)}, f32[8,8,4,384]{3,2,1,0:T(4,128)S(1)}) fusion(f32[8,8,24,384]{3,2,1,0:T(8,128)} %param.5), kind=kLoop, calls=%fused_computation.83 | loop fusion | bytes 1572864 | tf_op jit(solution)/shard_map/slice | solution.py:13
  12.5 1.8 %collective-permute-start = (f32[8,8,4,384]{3,1,2,0:T(8,128)S(1)}, f32[8,8,4,384]{3,1,2,0:T(8,128)S(1)}, u32[]{:S(2)}, u32[]{:S(2)}) collective-permute-start(f32[8,8,4,384]{3,1,2,0:T(8,128)S(1)} %copy.29), channel_id=1, source_target_pairs={{0,1},{1,2},{2,3},{3,4},{4,5},{5,6},{6,7},{7,0},{8,9},{9,10},{10,1... | collective-permute-start | bytes 1179656 | tf_op jit(solution)/shard_map/ppermute | solution.py:16
  15.5 0.8 slice_bitcast_fusion.2
  16.2 0.8 slice_bitcast_fusion.3
  17.8 0.8 slice_bitcast_fusion.1
  18.7 2.6 %collective-permute-done = f32[8,8,4,384]{3,1,2,0:T(8,128)S(1)} collective-permute-done((f32[8,8,4,384]{3,1,2,0:T(8,128)S(1)}, f32[8,8,4,384]{3,1,2,0:T(8,128)S(1)}, u32[]{:S(2)}, u32[]{:S(2)}) %collective-permute-start) | collective-permute-done | bytes 393248 | tf_op jit(solution)/shard_map/ppermute | solution.py:16
  21.4 4.5 %collective-permute-done.1 = f32[8,8,4,384]{3,1,2,0:T(8,128)S(1)} collective-permute-done((f32[8,8,4,384]{3,1,2,0:T(8,128)S(1)}, f32[8,8,4,384]{3,1,2,0:T(8,128)S(1)}, u32[]{:S(2)}, u32[]{:S(2)}) %collective-permute-start.1) | collective-permute-done | bytes 393248 | tf_op jit(solution)/shard_map/ppermute | solution.py:18
  26.5 1.2 fusion.24
  28.2 1.7 %fusion.26 = f32[8,8,30,384]{3,2,1,0:T(8,128)S(1)} fusion(f32[8,8,31,384]{3,2,1,0:T(8,128)S(1)} %fusion.27, f32[8,8,32,384]{3,2,1,0:T(8,128)S(1)} %pad_maximum_fusion, f32[8,8,30,383]{3,2,1,0:T(8,128)S(1)} %fusion.24), kind=kLoop, calls=%fused_computation.52 | loop fusion | flops 2949120 | bytes 14737920 | tf_op jit(solution)/shard_map/sub | solution.py:36
  29.9 1.2 fusion.20
  31.7 1.7 %fusion.22 = f32[8,8,28,384]{3,2,1,0:T(8,128)S(1)} fusion(f32[8,8,29,384]{3,2,1,0:T(8,128)S(1)} %fusion.23, f32[8,8,30,384]{3,2,1,0:T(8,128)S(1)} %fusion.26, f32[8,8,28,383]{3,2,1,0:T(8,128)S(1)} %fusion.20), kind=kLoop, calls=%fused_computation.44 | loop fusion | flops 2752512 | bytes 13755392 | tf_op jit(solution)/shard_map/sub | solution.py:36
  33.4 1.2 fusion.16
  35.2 1.7 %fusion.18 = f32[8,8,26,384]{3,2,1,0:T(8,128)S(1)} fusion(f32[8,8,27,384]{3,2,1,0:T(8,128)S(1)} %fusion.19, f32[8,8,28,384]{3,2,1,0:T(8,128)S(1)} %fusion.22, f32[8,8,26,383]{3,2,1,0:T(8,128)S(1)} %fusion.16), kind=kLoop, calls=%fused_computation.36 | loop fusion | flops 2555904 | bytes 12772864 | tf_op jit(solution)/shard_map/sub | solution.py:36
  37.8 1.1 fusion.32
  38.9 1.2 fusion.34
  40.6 1.3 fusion
  41.9 50.4 %all-gather.3.cloned.1.call-done = f32[8,8,24,384]{3,2,1,0:T(8,128)} async-done(((f32[2,8,24,384]{3,2,1,0:T(8,128)}), f32[8,8,24,384]{3,2,1,0:T(8,128)}) %all-gather.3.cloned.1.call-update) | async-done | bytes 2359312 | tf_op jit(solution)/shard_map/all_gather | solution.py:47
  92.3 2.7 %reduce_sum.28 = f32[2,8,24,384]{3,2,1,0:T(8,128)} reduce(f32[4,2,8,24,384]{4,3,2,1,0:T(8,128)} %bitcast.29, f32[]{:T(128)} %constant.1.clone.1), dimensions={0}, to_apply=%region_1.0 | reduce | flops 442368 | bytes 2949124 | tf_op jit(solution)/shard_map/reduce_sum | solution.py:47
  95.0 1.6 %subtract_multiply_fusion = f32[2,8,24,384]{3,2,1,0:T(8,128)S(1)} fusion(f32[2,8,24,384]{3,2,1,0:T(8,128)} %param.8, f32[2,8,24,384]{3,2,1,0:T(8,128)} %reduce_sum.28, f32[2,8,24,384]{3,2,1,0:T(8,128)} %param.7), kind=kLoop, calls=%fused_computation.72 | loop fusion | flops 294912 | bytes 2359296 | tf_op jit(solution)/shard_map/mul | solution.py:50
  97.9 2.0 %collective-permute-start.4 = (f32[8,8,4,384]{3,1,2,0:T(8,128)S(1)}, f32[8,8,4,384]{3,1,2,0:T(8,128)S(1)}, u32[]{:S(2)}, u32[]{:S(2)}) collective-permute-start(f32[8,8,4,384]{3,1,2,0:T(8,128)S(1)} %copy.25), channel_id=1, source_target_pairs={{0,1},{1,2},{2,3},{3,4},{4,5},{5,6},{6,7},{7,0},{8,9},{9,10},{10,1... | collective-permute-start | bytes 1179656 | tf_op jit(solution)/shard_map/ppermute | solution.py:16
  100.0 7.0 %collective-permute-done.4 = f32[8,8,4,384]{3,1,2,0:T(8,128)S(1)} collective-permute-done((f32[8,8,4,384]{3,1,2,0:T(8,128)S(1)}, f32[8,8,4,384]{3,1,2,0:T(8,128)S(1)}, u32[]{:S(2)}, u32[]{:S(2)}) %collective-permute-start.4) | collective-permute-done | bytes 393248 | tf_op jit(solution)/shard_map/ppermute | solution.py:16
  107.1 3.4 %collective-permute-done.5 = f32[8,8,4,384]{3,1,2,0:T(8,128)S(1)} collective-permute-done((f32[8,8,4,384]{3,1,2,0:T(8,128)S(1)}, f32[8,8,4,384]{3,1,2,0:T(8,128)S(1)}, u32[]{:S(2)}, u32[]{:S(2)}) %collective-permute-start.5) | collective-permute-done | bytes 393248 | tf_op jit(solution)/shard_map/ppermute | solution.py:18
  111.5 1.2 fusion.11
  113.2 1.7 %fusion.13 = f32[8,8,30,384]{3,2,1,0:T(8,128)S(1)} fusion(f32[8,8,31,384]{3,2,1,0:T(8,128)S(1)} %fusion.14, f32[8,8,32,384]{3,2,1,0:T(8,128)S(1)} %pad_maximum_fusion.1, f32[8,8,30,383]{3,2,1,0:T(8,128)S(1)} %fusion.11), kind=kLoop, calls=%fused_computation.26 | loop fusion | flops 2949120 | bytes 14737920 | tf_op jit(solution)/shard_map/sub | solution.py:36
  115.0 1.2 fusion.7
  116.7 1.7 %fusion.9 = f32[8,8,28,384]{3,2,1,0:T(8,128)S(1)} fusion(f32[8,8,29,384]{3,2,1,0:T(8,128)S(1)} %fusion.10, f32[8,8,30,384]{3,2,1,0:T(8,128)S(1)} %fusion.13, f32[8,8,28,383]{3,2,1,0:T(8,128)S(1)} %fusion.7), kind=kLoop, calls=%fused_computation.18 | loop fusion | flops 2752512 | bytes 13755392 | tf_op jit(solution)/shard_map/sub | solution.py:36
  118.4 1.2 fusion.3
  120.2 1.7 %fusion.5 = f32[8,8,26,384]{3,2,1,0:T(8,128)S(1)} fusion(f32[8,8,27,384]{3,2,1,0:T(8,128)S(1)} %fusion.6, f32[8,8,28,384]{3,2,1,0:T(8,128)S(1)} %fusion.9, f32[8,8,26,383]{3,2,1,0:T(8,128)S(1)} %fusion.3), kind=kLoop, calls=%fused_computation.10 | loop fusion | flops 2555904 | bytes 12772864 | tf_op jit(solution)/shard_map/sub | solution.py:36
  122.8 0.9 fusion.28
  123.8 2.9 %fusion.31 = f32[8,8,24,384]{3,2,1,0:T(8,128)} fusion(f32[8,8,24,384]{3,2,1,0:T(8,128)S(1)} %copy-done, f32[8,8,25,384]{3,2,1,0:T(8,128)S(1)} %fusion.2, f32[8,8,26,384]{3,2,1,0:T(8,128)S(1)} %fusion.5, f32[8,8,24,383]{3,2,1,0:T(8,128)S(1)} %fusion.28), kind=kLoop, calls=%fused_computation.63 | loop fusion | flops 2949120 | bytes 14149632 | tf_op jit(solution)/shard_map/add | solution.py:54
  (65 shorter events, 10.8 us)
Async XLA Ops:
  7.2 7.3 %copy-start.3 = (f32[2,8,24,384]{3,2,1,0:T(8,128)S(1)}, f32[2,8,24,384]{3,2,1,0:T(8,128)}, u32[]{:S(2)}) copy-start(f32[2,8,24,384]{3,2,1,0:T(8,128)} %param.9) | copy-start | bytes 1769476
  7.2 85.1 %all-gather.3.cloned.1.call-start = ((), (), s32[]{:S(2)}) async-start(), calls=%async_computation | async-start | bytes 2949120 | tf_op jit(solution)/shard_map/all_gather | solution.py:47
  8.3 6.9 %collective-permute-start.2 = (f32[2,8,4,384]{3,2,1,0:T(4,128)S(1)}, f32[2,8,4,384]{3,2,1,0:T(4,128)S(1)}, u32[]{:S(2)}, u32[]{:S(2)}) collective-permute-start(f32[2,8,4,384]{3,2,1,0:T(4,128)S(1)} %get-tuple-element.8), channel_id=1, source_target_pairs={{0,1},{1,2},{2,3},{3,4},{4,5},{5,6},{6,7},{7,0},{8,9},{9,10},{10,1... | collective-permute-start | bytes 294920 | tf_op jit(solution)/shard_map/ppermute | solution.py:16
  11.0 4.3 %collective-permute-start.3 = (f32[2,8,4,384]{3,2,1,0:T(4,128)S(1)}, f32[2,8,4,384]{3,2,1,0:T(4,128)S(1)}, u32[]{:S(2)}, u32[]{:S(2)}) collective-permute-start(f32[2,8,4,384]{3,2,1,0:T(4,128)S(1)} %get-tuple-element.9), channel_id=1, source_target_pairs={{1,0},{2,1},{3,2},{4,3},{5,4},{6,5},{7,6},{0,7},{9,8},{10,9},{11,1... | collective-permute-start | bytes 294920 | tf_op jit(solution)/shard_map/ppermute | solution.py:18
  12.5 8.7 %collective-permute-start = (f32[8,8,4,384]{3,1,2,0:T(8,128)S(1)}, f32[8,8,4,384]{3,1,2,0:T(8,128)S(1)}, u32[]{:S(2)}, u32[]{:S(2)}) collective-permute-start(f32[8,8,4,384]{3,1,2,0:T(8,128)S(1)} %copy.29), channel_id=1, source_target_pairs={{0,1},{1,2},{2,3},{3,4},{4,5},{5,6},{6,7},{7,0},{8,9},{9,10},{10,1... | collective-permute-start | bytes 1179656 | tf_op jit(solution)/shard_map/ppermute | solution.py:16
  14.4 11.5 %collective-permute-start.1 = (f32[8,8,4,384]{3,1,2,0:T(8,128)S(1)}, f32[8,8,4,384]{3,1,2,0:T(8,128)S(1)}, u32[]{:S(2)}, u32[]{:S(2)}) collective-permute-start(f32[8,8,4,384]{3,1,2,0:T(8,128)S(1)} %copy.30), channel_id=1, source_target_pairs={{1,0},{2,1},{3,2},{4,3},{5,4},{6,5},{7,6},{0,7},{9,8},{10,9},{11,1... | collective-permute-start | bytes 1179656 | tf_op jit(solution)/shard_map/ppermute | solution.py:18
  15.4 11.1 %copy-start.12 = (f32[8,30,384]{2,1,0:T(8,128)}, f32[8,30,384]{2,1,0:T(8,128)S(1)}, u32[]{:S(2)}) copy-start(f32[8,30,384]{2,1,0:T(8,128)S(1)} %slice_bitcast_fusion.4) | copy-start | bytes 1105924
  15.4 10.5 %copy-start = (f32[8,8,24,384]{3,2,1,0:T(8,128)S(1)}, f32[8,8,24,384]{3,2,1,0:T(8,128)}, u32[]{:S(2)}) copy-start(f32[8,8,24,384]{3,2,1,0:T(8,128)} %param.5) | copy-start | bytes 7077892
  15.5 12.2 %copy-start.10 = (f32[8,31,384]{2,1,0:T(8,128)}, f32[8,31,384]{2,1,0:T(8,128)S(1)}, u32[]{:S(2)}) copy-start(f32[8,31,384]{2,1,0:T(8,128)S(1)} %slice_bitcast_fusion.5) | copy-start | bytes 1142788
  28.2 1.7 %copy-start.9 = (f32[8,28,384]{2,1,0:T(8,128)S(1)}, f32[8,28,384]{2,1,0:T(8,128)}, u32[]{:S(2)}) copy-start(f32[8,28,384]{2,1,0:T(8,128)} %slice_bitcast_fusion.2) | copy-start | bytes 1032196
  29.9 1.2 copy-start.7
  31.7 1.7 %copy-start.4 = (f32[8,26,384]{2,1,0:T(8,128)S(1)}, f32[8,26,384]{2,1,0:T(8,128)}, u32[]{:S(2)}) copy-start(f32[8,26,384]{2,1,0:T(8,128)} %slice_bitcast_fusion) | copy-start | bytes 958468
  33.4 1.2 copy-start.5
  36.9 1.0 copy-start.14
  38.9 1.7 %copy-start.1 = (bf16[2,8,8,24,384]{4,3,2,1,0:T(8,128)(2,1)S(1)}, bf16[2,8,8,24,384]{4,3,2,1,0:T(8,128)(2,1)}, u32[]{:S(2)}) copy-start(bf16[2,8,8,24,384]{4,3,2,1,0:T(8,128)(2,1)} %param.6) | copy-start | bytes 7077892
  95.0 2.2 %copy-start.2 = (bf16[2,8,8,24,384]{4,3,2,1,0:T(8,128)(2,1)S(1)}, bf16[2,8,8,24,384]{4,3,2,1,0:T(8,128)(2,1)}, u32[]{:S(2)}) copy-start(bf16[2,8,8,24,384]{4,3,2,1,0:T(8,128)(2,1)} %param.6) | copy-start | bytes 7077892
  97.9 9.1 %collective-permute-start.4 = (f32[8,8,4,384]{3,1,2,0:T(8,128)S(1)}, f32[8,8,4,384]{3,1,2,0:T(8,128)S(1)}, u32[]{:S(2)}, u32[]{:S(2)}) collective-permute-start(f32[8,8,4,384]{3,1,2,0:T(8,128)S(1)} %copy.25), channel_id=1, source_target_pairs={{0,1},{1,2},{2,3},{3,4},{4,5},{5,6},{6,7},{7,0},{8,9},{9,10},{10,1... | collective-permute-start | bytes 1179656 | tf_op jit(solution)/shard_map/ppermute | solution.py:16
  99.9 10.5 %collective-permute-start.5 = (f32[8,8,4,384]{3,1,2,0:T(8,128)S(1)}, f32[8,8,4,384]{3,1,2,0:T(8,128)S(1)}, u32[]{:S(2)}, u32[]{:S(2)}) collective-permute-start(f32[8,8,4,384]{3,1,2,0:T(8,128)S(1)} %copy.26), channel_id=1, source_target_pairs={{1,0},{2,1},{3,2},{4,3},{5,4},{6,5},{7,6},{0,7},{9,8},{10,9},{11,1... | collective-permute-start | bytes 1179656 | tf_op jit(solution)/shard_map/ppermute | solution.py:18
  110.5 1.0 copy-start.13
  111.5 1.2 copy-start.11
  115.0 1.2 copy-start.8
  118.4 1.2 copy-start.6
  121.9 1.0 copy-start.15
Sparse Core Ops, SparseCore 0:
  42.1 50.1 all-gather.2
